TPU v7x, 32 devices: a whole 2x2x4 slice. The times are simulated.
32 devices in a mesh: row: 2 (over x), col: 16 (over z, y, core).
Axes of the slice: x: 2, y: 2, z: 4, core: 2. Of those that a mesh axis runs over, the one named last changes fastest.
Arguments:
- features: bfloat16 [8192, 256], P(('row', 'col')), may hold values from -6 to 6
- weight: bfloat16 [256, 128], replicated, may hold values from -0.375 to 0.375
- tiles: bfloat16 [2, 16, 320, 128, 128], P('row', 'col'), may hold values from -0.0625 to 0.0625
- slot_tile_row: int32 [2, 16, 320], P('row', 'col'), may hold values from 0 to 3
- tile_cols: int32 [2, 16, 320], P('row', 'col'), may hold values from 0 to 31
- live_tiles: int32 [2, 16], P('row', 'col'), may hold values from 40 to 320, as said below
- cotangent: bfloat16 [8192, 128], P(('row', 'col')), may hold values from -6 to 6
Outputs:
- logits: bfloat16 [8192, 128], P(('row', 'col'))
- grad_features: bfloat16 [8192, 256], P(('row', 'col'))
- grad_weight: float32 [256, 128], replicated
Inputs may be any that keep to these rules, and one draw needn't show every extreme that they name: Slots of a block from live_tiles on are padding and not part of the adjacency; in every draw some block has all 320 slots live.
All inputs are finite; a program needn't handle non-finite values.
Results may differ from a plain program's by a relative error of at most 0.005.
Values may be sent and summed in bfloat16 or wider, within the bound.
A program may use at most 128 MiB of HBM per device.

v0:
```python
import math
import jax
import jax.numpy as jnp
from jax import lax
from jax.sharding import PartitionSpec as P


def per_device(features, weight, tiles, slot_tile_row, tile_cols, live_tiles, cotangent):
    tile_block = tiles[0, 0]
    slot_rows = slot_tile_row[0, 0]
    slot_cols = tile_cols[0, 0]
    live_count = live_tiles[0, 0]
    tile_extent = tile_block.shape[-1]
    slot_total = tile_block.shape[0]
    stretch_rows = features.shape[0]
    output_width = weight.shape[1]
    row_count = lax.axis_size("row")
    col_count = lax.axis_size("col")
    row_tiles = row_count * stretch_rows // tile_extent
    col_tiles = col_count * stretch_rows // tile_extent
    block_size = 64
    block_total = slot_total // block_size
    projected_group = jnp.dot(
        lax.all_gather(features, "col", axis=0, tiled=True),
        weight,
        preferred_element_type=jnp.float32,
    ).astype(jnp.bfloat16)
    proj_tiles = projected_group.reshape(col_tiles, tile_extent, output_width)

    def block_slice(first_slot):
        part_tiles = lax.dynamic_slice_in_dim(tile_block, first_slot, block_size, 0)
        part_rows = lax.dynamic_slice_in_dim(slot_rows, first_slot, block_size, 0)
        part_cols = lax.dynamic_slice_in_dim(slot_cols, first_slot, block_size, 0)
        live_mask = first_slot + jnp.arange(block_size, dtype=jnp.int32) < live_count
        return (part_tiles, part_rows, part_cols, live_mask)

    def forward_block(block_index, totals):
        part_tiles, part_rows, part_cols, live_mask = block_slice(block_index * block_size)
        inputs = proj_tiles[part_cols]
        products = jnp.einsum(
            "tab,tbf->taf", part_tiles, inputs, preferred_element_type=jnp.float32
        )
        segment_ids = jnp.where(live_mask, part_rows, row_tiles)
        summed = jax.ops.segment_sum(products, segment_ids, num_segments=row_tiles + 1)
        return totals + summed[:row_tiles]

    forward_totals = lax.fori_loop(
        0,
        block_total,
        forward_block,
        jnp.zeros((row_tiles, tile_extent, output_width), jnp.float32),
    )
    logits = lax.psum_scatter(
        forward_totals.reshape(row_tiles * tile_extent, output_width),
        "row",
        scatter_dimension=0,
        tiled=True,
    ).astype(jnp.bfloat16)
    cot_group = lax.all_gather(cotangent, "row", axis=0, tiled=True)
    cot_tiles = cot_group.reshape(row_tiles, tile_extent, output_width)

    def backward_block(block_index, totals):
        part_tiles, part_rows, part_cols, live_mask = block_slice(block_index * block_size)
        inputs = cot_tiles[part_rows]
        products = jnp.einsum(
            "tab,taf->tbf", part_tiles, inputs, preferred_element_type=jnp.float32
        )
        inside = live_mask & (part_cols >= 0) & (part_cols < col_tiles)
        segment_ids = jnp.where(inside, part_cols, col_tiles)
        summed = jax.ops.segment_sum(products, segment_ids, num_segments=col_tiles + 1)
        return totals + summed[:col_tiles]

    empty = jnp.zeros((col_tiles, tile_extent, output_width), jnp.float32)
    backward_totals = lax.fori_loop(0, block_total, backward_block, empty).reshape(
        col_tiles * tile_extent, output_width
    )
    back = lax.psum_scatter(backward_totals, "col", scatter_dimension=0, tiled=True)
    back_rounded = back.astype(jnp.bfloat16)
    grad_features = jnp.dot(back_rounded, weight.T, preferred_element_type=jnp.float32).astype(
        jnp.bfloat16
    )
    weight_term = lax.dot_general(
        features, back_rounded, (((0,), (0,)), ((), ())), preferred_element_type=jnp.float32
    )
    node_total = stretch_rows * row_count * col_count
    grad_weight = lax.psum(weight_term, ("row", "col")) / math.sqrt(node_total)
    return (logits, grad_features, grad_weight)


def solution(mesh):
    placed = (
        P(("row", "col"), None),
        P(),
        P("row", "col", None, None, None),
        P("row", "col", None),
        P("row", "col", None),
        P("row", "col"),
        P(("row", "col"), None),
    )
    return jax.shard_map(
        per_device,
        mesh=mesh,
        in_specs=placed,
        out_specs=(P(("row", "col"), None), P(("row", "col"), None), P()),
        check_vma=False,
    )
```

profile of v0, /device:TPU:0, one launch (start us, length us, event | category | flops | bytes accessed | tf_op | source)
XLA Modules:
  0.0 375.7 jit_solution(15768739046971264460)
XLA Ops:
  8.6 14.4 %copy.10 = bf16[1,1,320,128,128]{3,4,2,1,0:T(8,128)(2,1)} copy(bf16[1,1,320,128,128]{4,3,2,1,0:T(8,128)(2,1)} %param.13) | data formatting | bytes 20971520 | tf_op args[2]
  23.0 5.9 %all_gather.7 = bf16[512,128]{1,0:T(8,128)(2,1)S(1)} all-gather(bf16[256,128]{1,0:T(8,128)(2,1)S(1)} %copy-done.3), channel_id=1, replica_groups=mesh['row'=2,'col'=16] {'row'}, dimensions={0}, use_global_device_ids=true | all-gather | bytes 196608 | tf_op jit(solution)/shard_map/all_gather | solution.py:59
  28.9 90.2 %while.29 = (s32[]{:T(128)}, f32[32,128,128]{2,1,0:T(8,128)}, s32[]{:T(128)}, s32[320]{0:T(512)S(1)}, bf16[320,128,128]{1,2,0:T(8,128)(2,1)}, /*index=5*/s32[320...) while((s32[]{:T(128)}, f32[32,128,128]{2,1,0:T(8,128)}, ...), condition=%wide.region_6.7_spmd.clone, body=%wide.region_4.6_spmd.clone.sunk | while | flops 270534272 | bytes 33626048 | solution.py:74
  30.6 4.4 %fusion.25 = f32[64,128,128]{2,1,0:T(8,128)} fusion(bf16[64,128,128]{2,1,0:T(8,128)(2,1)S(1)} %gather_fusion.1, bf16[320,128,128]{1,2,0:T(8,128)(2,1)} %get-tuple-element.501, s32[]{:T(128)S(6)} %select_n.64), kind=kOutput, calls=%fused_computation.12.clone.1 | convolution fusion | flops 268435456 | bytes 8388612 | tf_op jit(solution)/shard_map/while/body/eval_jaxpr/tab,taf->tbf/dot_general | solution.py:65
  35.2 8.8 %scatter_fusion.1 = f32[33,128,128]{2,1,0:T(8,128)S(1)} fusion(f32[33,128,128]{2,1,0:T(8,128)S(1)} %broadcast.112, s32[64]{0:T(128)S(1)} %get-tuple-element.435, f32[64,128,128]{2,1,0:T(8,128)} %fusion.25), kind=kCustom, calls=%fused_computation.3.clone.clone.1 | custom fusion | flops 1048576 | bytes 12583168 | tf_op jit(solution)/shard_map/while/body/eval_jaxpr/scatter-add | solution.py:70
  47.4 4.4 %fusion.25 = f32[64,128,128]{2,1,0:T(8,128)} fusion(bf16[64,128,128]{2,1,0:T(8,128)(2,1)S(1)} %gather_fusion.1, bf16[320,128,128]{1,2,0:T(8,128)(2,1)} %get-tuple-element.501, s32[]{:T(128)S(6)} %select_n.64), kind=kOutput, calls=%fused_computation.12.clone.1 | convolution fusion | flops 268435456 | bytes 8388612 | tf_op jit(solution)/shard_map/while/body/eval_jaxpr/tab,taf->tbf/dot_general | solution.py:65
  52.0 8.8 %scatter_fusion.1 = f32[33,128,128]{2,1,0:T(8,128)S(1)} fusion(f32[33,128,128]{2,1,0:T(8,128)S(1)} %broadcast.112, s32[64]{0:T(128)S(1)} %get-tuple-element.435, f32[64,128,128]{2,1,0:T(8,128)} %fusion.25), kind=kCustom, calls=%fused_computation.3.clone.clone.1 | custom fusion | flops 1048576 | bytes 12583168 | tf_op jit(solution)/shard_map/while/body/eval_jaxpr/scatter-add | solution.py:70
  60.8 3.2 slice_add_fusion.5
  65.7 4.4 %fusion.25 = f32[64,128,128]{2,1,0:T(8,128)} fusion(bf16[64,128,128]{2,1,0:T(8,128)(2,1)S(1)} %gather_fusion.1, bf16[320,128,128]{1,2,0:T(8,128)(2,1)} %get-tuple-element.501, s32[]{:T(128)S(6)} %select_n.64), kind=kOutput, calls=%fused_computation.12.clone.1 | convolution fusion | flops 268435456 | bytes 8388612 | tf_op jit(solution)/shard_map/while/body/eval_jaxpr/tab,taf->tbf/dot_general | solution.py:65
  70.3 8.8 %scatter_fusion.1 = f32[33,128,128]{2,1,0:T(8,128)S(1)} fusion(f32[33,128,128]{2,1,0:T(8,128)S(1)} %broadcast.112, s32[64]{0:T(128)S(1)} %get-tuple-element.435, f32[64,128,128]{2,1,0:T(8,128)} %fusion.25), kind=kCustom, calls=%fused_computation.3.clone.clone.1 | custom fusion | flops 1048576 | bytes 12583168 | tf_op jit(solution)/shard_map/while/body/eval_jaxpr/scatter-add | solution.py:70
  79.2 3.2 slice_add_fusion.5
  84.1 4.4 %fusion.25 = f32[64,128,128]{2,1,0:T(8,128)} fusion(bf16[64,128,128]{2,1,0:T(8,128)(2,1)S(1)} %gather_fusion.1, bf16[320,128,128]{1,2,0:T(8,128)(2,1)} %get-tuple-element.501, s32[]{:T(128)S(6)} %select_n.64), kind=kOutput, calls=%fused_computation.12.clone.1 | convolution fusion | flops 268435456 | bytes 8388612 | tf_op jit(solution)/shard_map/while/body/eval_jaxpr/tab,taf->tbf/dot_general | solution.py:65
  88.7 8.8 %scatter_fusion.1 = f32[33,128,128]{2,1,0:T(8,128)S(1)} fusion(f32[33,128,128]{2,1,0:T(8,128)S(1)} %broadcast.112, s32[64]{0:T(128)S(1)} %get-tuple-element.435, f32[64,128,128]{2,1,0:T(8,128)} %fusion.25), kind=kCustom, calls=%fused_computation.3.clone.clone.1 | custom fusion | flops 1048576 | bytes 12583168 | tf_op jit(solution)/shard_map/while/body/eval_jaxpr/scatter-add | solution.py:70
  97.5 3.2 slice_add_fusion.5
  102.4 4.4 %fusion.25 = f32[64,128,128]{2,1,0:T(8,128)} fusion(bf16[64,128,128]{2,1,0:T(8,128)(2,1)S(1)} %gather_fusion.1, bf16[320,128,128]{1,2,0:T(8,128)(2,1)} %get-tuple-element.501, s32[]{:T(128)S(6)} %select_n.64), kind=kOutput, calls=%fused_computation.12.clone.1 | convolution fusion | flops 268435456 | bytes 8388612 | tf_op jit(solution)/shard_map/while/body/eval_jaxpr/tab,taf->tbf/dot_general | solution.py:65
  107.1 8.8 %scatter_fusion.1 = f32[33,128,128]{2,1,0:T(8,128)S(1)} fusion(f32[33,128,128]{2,1,0:T(8,128)S(1)} %broadcast.112, s32[64]{0:T(128)S(1)} %get-tuple-element.435, f32[64,128,128]{2,1,0:T(8,128)} %fusion.25), kind=kCustom, calls=%fused_computation.3.clone.clone.1 | custom fusion | flops 1048576 | bytes 12583168 | tf_op jit(solution)/shard_map/while/body/eval_jaxpr/scatter-add | solution.py:70
  115.9 3.2 slice_add_fusion.5
  119.9 62.9 %reduce-scatter.5.cloned.1.call-done = f32[256,128]{1,0:T(8,128)} async-done(((f32[4096,128]{1,0:T(8,128)}), f32[256,128]{1,0:T(8,128)}) %reduce-scatter.5.cloned.1.call-update) | async-done | bytes 131088 | tf_op jit(solution)/shard_map/reduce_scatter | solution.py:77
  184.6 40.8 %all-gather.2.cloned.1.call-done = bf16[4096,256]{1,0:T(8,128)(2,1)} async-done(((bf16[256,256]{1,0:T(8,128)(2,1)}), bf16[4096,256]{1,0:T(8,128)(2,1)}) %all-gather.2.cloned.1.call-update) | async-done | bytes 2097168 | tf_op jit(solution)/shard_map/all_gather | solution.py:24
  227.7 74.2 %while.28 = (s32[]{:T(128)}, f32[4,128,128]{2,1,0:T(8,128)S(1)}, s32[]{:T(128)}, s32[320]{0:T(512)S(1)}, bf16[320,128,128]{2,1,0:T(8,128)(2,1)}, /*index=5*/s32[...) while((s32[]{:T(128)}, f32[4,128,128]{2,1,0:T(8,128)S(1)}, ...), condition=%wide.region_2.3_spmd.clone, body=%wide.region_0.2_spmd.clone.sunk | while | flops 269616512 | bytes 26286016 | solution.py:47
  229.4 4.2 %fusion.22 = f32[64,128,128]{2,1,0:T(8,128)} fusion(bf16[64,128,128]{2,1,0:T(8,128)(2,1)S(1)} %gather_fusion, bf16[320,128,128]{2,1,0:T(8,128)(2,1)} %get-tuple-element.465, s32[]{:T(128)S(6)} %select_n.62), kind=kOutput, calls=%fused_computation.4.clone.1 | convolution fusion | flops 268435456 | bytes 8388612 | tf_op jit(solution)/shard_map/while/body/eval_jaxpr/tab,tbf->taf/dot_general | solution.py:40
  233.7 8.8 %scatter_fusion = f32[5,128,128]{2,1,0:T(8,128)S(1)} fusion(f32[5,128,128]{2,1,0:T(8,128)S(1)} %broadcast.105, s32[64]{0:T(128)S(1)} %get-tuple-element.426, f32[64,128,128]{2,1,0:T(8,128)} %fusion.22), kind=kCustom, calls=%fused_computation.2.clone.clone.1 | custom fusion | flops 1048576 | bytes 12583168 | tf_op jit(solution)/shard_map/while/body/eval_jaxpr/scatter-add | solution.py:44
  244.2 4.2 %fusion.22 = f32[64,128,128]{2,1,0:T(8,128)} fusion(bf16[64,128,128]{2,1,0:T(8,128)(2,1)S(1)} %gather_fusion, bf16[320,128,128]{2,1,0:T(8,128)(2,1)} %get-tuple-element.465, s32[]{:T(128)S(6)} %select_n.62), kind=kOutput, calls=%fused_computation.4.clone.1 | convolution fusion | flops 268435456 | bytes 8388612 | tf_op jit(solution)/shard_map/while/body/eval_jaxpr/tab,tbf->taf/dot_general | solution.py:40
  248.5 8.8 %scatter_fusion = f32[5,128,128]{2,1,0:T(8,128)S(1)} fusion(f32[5,128,128]{2,1,0:T(8,128)S(1)} %broadcast.105, s32[64]{0:T(128)S(1)} %get-tuple-element.426, f32[64,128,128]{2,1,0:T(8,128)} %fusion.22), kind=kCustom, calls=%fused_computation.2.clone.clone.1 | custom fusion | flops 1048576 | bytes 12583168 | tf_op jit(solution)/shard_map/while/body/eval_jaxpr/scatter-add | solution.py:44
  259.1 4.2 %fusion.22 = f32[64,128,128]{2,1,0:T(8,128)} fusion(bf16[64,128,128]{2,1,0:T(8,128)(2,1)S(1)} %gather_fusion, bf16[320,128,128]{2,1,0:T(8,128)(2,1)} %get-tuple-element.465, s32[]{:T(128)S(6)} %select_n.62), kind=kOutput, calls=%fused_computation.4.clone.1 | convolution fusion | flops 268435456 | bytes 8388612 | tf_op jit(solution)/shard_map/while/body/eval_jaxpr/tab,tbf->taf/dot_general | solution.py:40
  263.4 8.8 %scatter_fusion = f32[5,128,128]{2,1,0:T(8,128)S(1)} fusion(f32[5,128,128]{2,1,0:T(8,128)S(1)} %broadcast.105, s32[64]{0:T(128)S(1)} %get-tuple-element.426, f32[64,128,128]{2,1,0:T(8,128)} %fusion.22), kind=kCustom, calls=%fused_computation.2.clone.clone.1 | custom fusion | flops 1048576 | bytes 12583168 | tf_op jit(solution)/shard_map/while/body/eval_jaxpr/scatter-add | solution.py:44
  273.9 4.2 %fusion.22 = f32[64,128,128]{2,1,0:T(8,128)} fusion(bf16[64,128,128]{2,1,0:T(8,128)(2,1)S(1)} %gather_fusion, bf16[320,128,128]{2,1,0:T(8,128)(2,1)} %get-tuple-element.465, s32[]{:T(128)S(6)} %select_n.62), kind=kOutput, calls=%fused_computation.4.clone.1 | convolution fusion | flops 268435456 | bytes 8388612 | tf_op jit(solution)/shard_map/while/body/eval_jaxpr/tab,tbf->taf/dot_general | solution.py:40
  278.2 8.8 %scatter_fusion = f32[5,128,128]{2,1,0:T(8,128)S(1)} fusion(f32[5,128,128]{2,1,0:T(8,128)S(1)} %broadcast.105, s32[64]{0:T(128)S(1)} %get-tuple-element.426, f32[64,128,128]{2,1,0:T(8,128)} %fusion.22), kind=kCustom, calls=%fused_computation.2.clone.clone.1 | custom fusion | flops 1048576 | bytes 12583168 | tf_op jit(solution)/shard_map/while/body/eval_jaxpr/scatter-add | solution.py:44
  288.8 4.2 %fusion.22 = f32[64,128,128]{2,1,0:T(8,128)} fusion(bf16[64,128,128]{2,1,0:T(8,128)(2,1)S(1)} %gather_fusion, bf16[320,128,128]{2,1,0:T(8,128)(2,1)} %get-tuple-element.465, s32[]{:T(128)S(6)} %select_n.62), kind=kOutput, calls=%fused_computation.4.clone.1 | convolution fusion | flops 268435456 | bytes 8388612 | tf_op jit(solution)/shard_map/while/body/eval_jaxpr/tab,tbf->taf/dot_general | solution.py:40
  293.1 8.8 %scatter_fusion = f32[5,128,128]{2,1,0:T(8,128)S(1)} fusion(f32[5,128,128]{2,1,0:T(8,128)S(1)} %broadcast.105, s32[64]{0:T(128)S(1)} %get-tuple-element.426, f32[64,128,128]{2,1,0:T(8,128)} %fusion.22), kind=kCustom, calls=%fused_computation.2.clone.clone.1 | custom fusion | flops 1048576 | bytes 12583168 | tf_op jit(solution)/shard_map/while/body/eval_jaxpr/scatter-add | solution.py:44
  304.4 50.3 %all-reduce.2.cloned.1.call-done = f32[256,128]{0,1:T(8,128)} async-done(((f32[256,128]{0,1:T(8,128)}), f32[256,128]{0,1:T(8,128)}) %all-reduce.2.cloned.1.call-update) | async-done | bytes 131088 | tf_op jit(solution)/shard_map/psum | solution.py:86
  356.4 11.2 %reduce-scatter.3.cloned.1.call-done = f32[256,128]{1,0:T(8,128)} async-done(((f32[512,128]{1,0:T(8,128)}), f32[256,128]{1,0:T(8,128)}) %reduce-scatter.3.cloned.1.call-update) | async-done | bytes 131088 | tf_op jit(solution)/shard_map/reduce_scatter | solution.py:53
  (72 shorter events, 32.2 us)
Async XLA Ops:
  7.2 218.2 %copy-start = (bf16[256,128]{1,0:T(8,128)(2,1)S(1)}, bf16[256,128]{1,0:T(8,128)(2,1)}, u32[]{:S(2)}) copy-start(bf16[256,128]{1,0:T(8,128)(2,1)} %param.12) | copy-start | bytes 196612
  7.2 175.6 %reduce-scatter.5.cloned.1.call-start = ((), (), s32[]{:S(2)}) async-start(), calls=%async_computation.4 | async-start | bytes 2228224 | tf_op jit(solution)/shard_map/reduce_scatter | solution.py:77
  8.6 14.4 %copy-start.3 = (bf16[256,128]{1,0:T(8,128)(2,1)S(1)}, bf16[256,128]{1,0:T(8,128)(2,1)}, u32[]{:S(2)}) copy-start(bf16[256,128]{1,0:T(8,128)(2,1)} %param.17) | copy-start | bytes 196612
  119.1 63.7 %copy-start.2 = (bf16[256,256]{1,0:T(8,128)(2,1)S(1)}, bf16[256,256]{1,0:T(8,128)(2,1)}, u32[]{:S(2)}) copy-start(bf16[256,256]{1,0:T(8,128)(2,1)} %param.11) | copy-start | bytes 393220
  119.1 106.3 %all-gather.2.cloned.1.call-start = ((), (), s32[]{:S(2)}) async-start(), calls=%async_computation.2 | async-start | bytes 2228224 | tf_op jit(solution)/shard_map/all_gather | solution.py:24
  119.9 234.9 %all-reduce.2.cloned.1.call-start = ((), (), s32[]{:S(2)}) async-start(), calls=%async_computation.5 | async-start | bytes 262144 | tf_op jit(solution)/shard_map/psum | solution.py:86
  184.6 183.1 %reduce-scatter.3.cloned.1.call-start = ((), (), s32[]{:S(2)}) async-start(), calls=%async_computation.3 | async-start | bytes 393216 | tf_op jit(solution)/shard_map/reduce_scatter | solution.py:53
  301.9 0.7 copy-start.1
Sparse Core Ops, SparseCore 0:
  119.3 63.4 reduce-scatter.4
  185.0 40.3 all-gather.1
  231.5 123.1 all-reduce.1
  356.8 10.7 reduce-scatter.2
where the time goes:
time: 378 us; the launch traced here: 376 us
  waiting for transfers between devices  166 us (44%)
  other arithmetic  114 us (30%)
  matrix products  48.8 us (13%)
  local copies, waits for them, and re-layouts  26.7 us (7%)
  between operations  13.8 us (4%)
  blocking collectives  5.85 us (2%)
    reduce_scatter x1, waiting for transfers between devices, per_device(): lax.psum_scatter(backward_totals, 'col', scatter_dimension=0, tiled=True)  62.9 us
    psum x1, waiting for transfers between devices, per_device(): grad_weight = lax.psum(weight_term, ('row', 'col')) / math.sqrt(node_total)  50.3 us
    scatter-add x5, other arithmetic, backward_block(): jax.ops.segment_sum(products, segment_ids, num_segments=col_tiles + 1)  44 us
    scatter-add x5, other arithmetic, forward_block(): jax.ops.segment_sum(products, segment_ids, num_segments=row_tiles + 1)  43.9 us
    all_gather x1, waiting for transfers between devices, per_device(): lax.all_gather(features, 'col', axis=0, tiled=True)  40.8 us
    dot_general x5, matrix products, backward_block(): jnp.einsum('tab,taf->tbf', part_tiles, inputs, preferred_element_type=jnp...  21.9 us
    dot_general x5, matrix products, forward_block(): jnp.einsum('tab,tbf->taf', part_tiles, inputs, preferred_element_type=jnp...  21.1 us
    unnamed x10, local copies, waits for them, and re-layouts  15.9 us
  transfers between devices with their start and end apart: 4, of which 4 were waited for; matrix products, arithmetic and copies ran while one was open for 22% of the time, Pallas kernels for 0%

commit v1 on v0

--- a/solution.py
+++ b/solution.py
@@ -1,8 +1,19 @@
+import functools
 import math
 import jax
 import jax.numpy as jnp
 from jax import lax
 from jax.sharding import PartitionSpec as P
+from jax.lax import psum
+
+
+def raise_page(local_values, mesh_ax, shard_axis):
+    for ix in (mesh_ax, shard_axis):
+        local_values = psum(local_values, ix)
+    return local_values
+
+
+_change_stages_all = functools.partial(raise_page, mesh_ax="col", shard_axis="row")
 
 
 def per_device(features, weight, tiles, slot_tile_row, tile_cols, live_tiles, cotangent):
@@ -83,7 +94,7 @@
         features, back_rounded, (((0,), (0,)), ((), ())), preferred_element_type=jnp.float32
     )
     node_total = stretch_rows * row_count * col_count
-    grad_weight = lax.psum(weight_term, ("row", "col")) / math.sqrt(node_total)
+    grad_weight = _change_stages_all(weight_term) / math.sqrt(node_total)
     return (logits, grad_features, grad_weight)
 
 

time: 378 us -> 418 us (1.11)
  waiting for transfers between devices: 166 us -> 205 us
    psum x1 -> x2, waiting for transfers between devices: 50.3 us -> 88.6 us  [raise_page(): local_values = psum(local_values, ix)]
    all_gather x1, waiting for transfers between devices: 40.8 us -> 45.1 us  [per_device(): lax.all_gather(features, 'col', axis=0, tiled=True)]
  transfers between devices with their start and end apart: 4 -> 5, of which waited for: 4 -> 4; matrix products, arithmetic and copies ran while one was open for 22% -> 19% of each run, Pallas kernels for 0% -> 0%
where the time goes in v1:
time: 418 us; the launch traced here: 415 us
  waiting for transfers between devices  205 us (49%)
  other arithmetic  114 us (27%)
  matrix products  48.8 us (12%)
  local copies, waits for them, and re-layouts  26.7 us (6%)
  between operations  13.8 us (3%)
  blocking collectives  5.85 us (1%)
    psum x2, waiting for transfers between devices, raise_page(): local_values = psum(local_values, ix)  88.6 us
    reduce_scatter x1, waiting for transfers between devices, per_device(): lax.psum_scatter(backward_totals, 'col', scatter_dimension=0, tiled=True)  63.6 us
    all_gather x1, waiting for transfers between devices, per_device(): lax.all_gather(features, 'col', axis=0, tiled=True)  45.1 us
    scatter-add x5, other arithmetic, backward_block(): jax.ops.segment_sum(products, segment_ids, num_segments=col_tiles + 1)  44 us
    scatter-add x5, other arithmetic, forward_block(): jax.ops.segment_sum(products, segment_ids, num_segments=row_tiles + 1)  43.9 us
    dot_general x5, matrix products, backward_block(): jnp.einsum('tab,taf->tbf', part_tiles, inputs, preferred_element_type=jnp...  21.9 us
    dot_general x5, matrix products, forward_block(): jnp.einsum('tab,tbf->taf', part_tiles, inputs, preferred_element_type=jnp...  21.1 us
    unnamed x10, local copies, waits for them, and re-layouts  15.9 us
  transfers between devices with their start and end apart: 5, of which 4 were waited for; matrix products, arithmetic and copies ran while one was open for 19% of the time, Pallas kernels for 0%

profile of v1, /device:TPU:0, one launch (start us, length us, event | category | flops | bytes accessed | tf_op | source)
XLA Modules:
  0.0 415.1 jit_solution(12953329961797786191)
XLA Ops:
  8.6 14.4 %copy.10 = bf16[1,1,320,128,128]{3,4,2,1,0:T(8,128)(2,1)} copy(bf16[1,1,320,128,128]{4,3,2,1,0:T(8,128)(2,1)} %param.13) | data formatting | bytes 20971520 | tf_op args[2]
  23.0 5.9 %all_gather.7 = bf16[512,128]{1,0:T(8,128)(2,1)S(1)} all-gather(bf16[256,128]{1,0:T(8,128)(2,1)S(1)} %copy-done.3), channel_id=1, replica_groups=mesh['row'=2,'col'=16] {'row'}, dimensions={0}, use_global_device_ids=true | all-gather | bytes 196608 | tf_op jit(solution)/shard_map/all_gather | solution.py:70
  28.9 90.2 %while.29 = (s32[]{:T(128)}, f32[32,128,128]{2,1,0:T(8,128)}, s32[]{:T(128)}, s32[320]{0:T(512)S(1)}, bf16[320,128,128]{1,2,0:T(8,128)(2,1)}, /*index=5*/s32[320...) while((s32[]{:T(128)}, f32[32,128,128]{2,1,0:T(8,128)}, ...), condition=%wide.region_6.7_spmd.clone, body=%wide.region_4.6_spmd.clone.sunk | while | flops 270534272 | bytes 33626048 | solution.py:85
  30.6 4.4 %fusion.25 = f32[64,128,128]{2,1,0:T(8,128)} fusion(bf16[64,128,128]{2,1,0:T(8,128)(2,1)S(1)} %gather_fusion.1, bf16[320,128,128]{1,2,0:T(8,128)(2,1)} %get-tuple-element.501, s32[]{:T(128)S(6)} %select_n.64), kind=kOutput, calls=%fused_computation.12.clone.1 | convolution fusion | flops 268435456 | bytes 8388612 | tf_op jit(solution)/shard_map/while/body/eval_jaxpr/tab,taf->tbf/dot_general | solution.py:76
  35.2 8.8 %scatter_fusion.1 = f32[33,128,128]{2,1,0:T(8,128)S(1)} fusion(f32[33,128,128]{2,1,0:T(8,128)S(1)} %broadcast.112, s32[64]{0:T(128)S(1)} %get-tuple-element.435, f32[64,128,128]{2,1,0:T(8,128)} %fusion.25), kind=kCustom, calls=%fused_computation.3.clone.clone.1 | custom fusion | flops 1048576 | bytes 12583168 | tf_op jit(solution)/shard_map/while/body/eval_jaxpr/scatter-add | solution.py:81
  47.4 4.4 %fusion.25 = f32[64,128,128]{2,1,0:T(8,128)} fusion(bf16[64,128,128]{2,1,0:T(8,128)(2,1)S(1)} %gather_fusion.1, bf16[320,128,128]{1,2,0:T(8,128)(2,1)} %get-tuple-element.501, s32[]{:T(128)S(6)} %select_n.64), kind=kOutput, calls=%fused_computation.12.clone.1 | convolution fusion | flops 268435456 | bytes 8388612 | tf_op jit(solution)/shard_map/while/body/eval_jaxpr/tab,taf->tbf/dot_general | solution.py:76
  52.0 8.8 %scatter_fusion.1 = f32[33,128,128]{2,1,0:T(8,128)S(1)} fusion(f32[33,128,128]{2,1,0:T(8,128)S(1)} %broadcast.112, s32[64]{0:T(128)S(1)} %get-tuple-element.435, f32[64,128,128]{2,1,0:T(8,128)} %fusion.25), kind=kCustom, calls=%fused_computation.3.clone.clone.1 | custom fusion | flops 1048576 | bytes 12583168 | tf_op jit(solution)/shard_map/while/body/eval_jaxpr/scatter-add | solution.py:81
  60.8 3.2 slice_add_fusion.5
  65.7 4.4 %fusion.25 = f32[64,128,128]{2,1,0:T(8,128)} fusion(bf16[64,128,128]{2,1,0:T(8,128)(2,1)S(1)} %gather_fusion.1, bf16[320,128,128]{1,2,0:T(8,128)(2,1)} %get-tuple-element.501, s32[]{:T(128)S(6)} %select_n.64), kind=kOutput, calls=%fused_computation.12.clone.1 | convolution fusion | flops 268435456 | bytes 8388612 | tf_op jit(solution)/shard_map/while/body/eval_jaxpr/tab,taf->tbf/dot_general | solution.py:76
  70.3 8.8 %scatter_fusion.1 = f32[33,128,128]{2,1,0:T(8,128)S(1)} fusion(f32[33,128,128]{2,1,0:T(8,128)S(1)} %broadcast.112, s32[64]{0:T(128)S(1)} %get-tuple-element.435, f32[64,128,128]{2,1,0:T(8,128)} %fusion.25), kind=kCustom, calls=%fused_computation.3.clone.clone.1 | custom fusion | flops 1048576 | bytes 12583168 | tf_op jit(solution)/shard_map/while/body/eval_jaxpr/scatter-add | solution.py:81
  79.2 3.2 slice_add_fusion.5
  84.1 4.4 %fusion.25 = f32[64,128,128]{2,1,0:T(8,128)} fusion(bf16[64,128,128]{2,1,0:T(8,128)(2,1)S(1)} %gather_fusion.1, bf16[320,128,128]{1,2,0:T(8,128)(2,1)} %get-tuple-element.501, s32[]{:T(128)S(6)} %select_n.64), kind=kOutput, calls=%fused_computation.12.clone.1 | convolution fusion | flops 268435456 | bytes 8388612 | tf_op jit(solution)/shard_map/while/body/eval_jaxpr/tab,taf->tbf/dot_general | solution.py:76
  88.7 8.8 %scatter_fusion.1 = f32[33,128,128]{2,1,0:T(8,128)S(1)} fusion(f32[33,128,128]{2,1,0:T(8,128)S(1)} %broadcast.112, s32[64]{0:T(128)S(1)} %get-tuple-element.435, f32[64,128,128]{2,1,0:T(8,128)} %fusion.25), kind=kCustom, calls=%fused_computation.3.clone.clone.1 | custom fusion | flops 1048576 | bytes 12583168 | tf_op jit(solution)/shard_map/while/body/eval_jaxpr/scatter-add | solution.py:81
  97.5 3.2 slice_add_fusion.5
  102.4 4.4 %fusion.25 = f32[64,128,128]{2,1,0:T(8,128)} fusion(bf16[64,128,128]{2,1,0:T(8,128)(2,1)S(1)} %gather_fusion.1, bf16[320,128,128]{1,2,0:T(8,128)(2,1)} %get-tuple-element.501, s32[]{:T(128)S(6)} %select_n.64), kind=kOutput, calls=%fused_computation.12.clone.1 | convolution fusion | flops 268435456 | bytes 8388612 | tf_op jit(solution)/shard_map/while/body/eval_jaxpr/tab,taf->tbf/dot_general | solution.py:76
  107.1 8.8 %scatter_fusion.1 = f32[33,128,128]{2,1,0:T(8,128)S(1)} fusion(f32[33,128,128]{2,1,0:T(8,128)S(1)} %broadcast.112, s32[64]{0:T(128)S(1)} %get-tuple-element.435, f32[64,128,128]{2,1,0:T(8,128)} %fusion.25), kind=kCustom, calls=%fused_computation.3.clone.clone.1 | custom fusion | flops 1048576 | bytes 12583168 | tf_op jit(solution)/shard_map/while/body/eval_jaxpr/scatter-add | solution.py:81
  115.9 3.2 slice_add_fusion.5
  119.2 63.6 %reduce-scatter.5.cloned.1.call-done = f32[256,128]{1,0:T(8,128)} async-done(((f32[4096,128]{1,0:T(8,128)}), f32[256,128]{1,0:T(8,128)}) %reduce-scatter.5.cloned.1.call-update) | async-done | bytes 131088 | tf_op jit(solution)/shard_map/reduce_scatter | solution.py:88
  185.4 88.6 %all-reduce.3.cloned.1.call-done = f32[256,128]{0,1:T(8,128)} async-done(((f32[256,128]{0,1:T(8,128)}), f32[256,128]{0,1:T(8,128)}) %all-reduce.3.cloned.1.call-update) | async-done | bytes 131088 | tf_op jit(solution)/shard_map/psum | solution.py:12
  274.1 45.1 %all-gather.2.cloned.1.call-done = bf16[4096,256]{1,0:T(8,128)(2,1)} async-done(((bf16[256,256]{1,0:T(8,128)(2,1)}), bf16[4096,256]{1,0:T(8,128)(2,1)}) %all-gather.2.cloned.1.call-update) | async-done | bytes 2097168 | tf_op jit(solution)/shard_map/all_gather | solution.py:35
  321.5 74.2 %while.28 = (s32[]{:T(128)}, f32[4,128,128]{2,1,0:T(8,128)S(1)}, s32[]{:T(128)}, s32[320]{0:T(512)S(1)}, bf16[320,128,128]{2,1,0:T(8,128)(2,1)}, /*index=5*/s32[...) while((s32[]{:T(128)}, f32[4,128,128]{2,1,0:T(8,128)S(1)}, ...), condition=%wide.region_2.3_spmd.clone, body=%wide.region_0.2_spmd.clone.sunk | while | flops 269616512 | bytes 26286016 | solution.py:58
  323.2 4.2 %fusion.22 = f32[64,128,128]{2,1,0:T(8,128)} fusion(bf16[64,128,128]{2,1,0:T(8,128)(2,1)S(1)} %gather_fusion, bf16[320,128,128]{2,1,0:T(8,128)(2,1)} %get-tuple-element.465, s32[]{:T(128)S(6)} %select_n.62), kind=kOutput, calls=%fused_computation.4.clone.1 | convolution fusion | flops 268435456 | bytes 8388612 | tf_op jit(solution)/shard_map/while/body/eval_jaxpr/tab,tbf->taf/dot_general | solution.py:51
  327.5 8.8 %scatter_fusion = f32[5,128,128]{2,1,0:T(8,128)S(1)} fusion(f32[5,128,128]{2,1,0:T(8,128)S(1)} %broadcast.105, s32[64]{0:T(128)S(1)} %get-tuple-element.426, f32[64,128,128]{2,1,0:T(8,128)} %fusion.22), kind=kCustom, calls=%fused_computation.2.clone.clone.1 | custom fusion | flops 1048576 | bytes 12583168 | tf_op jit(solution)/shard_map/while/body/eval_jaxpr/scatter-add | solution.py:55
  338.1 4.2 %fusion.22 = f32[64,128,128]{2,1,0:T(8,128)} fusion(bf16[64,128,128]{2,1,0:T(8,128)(2,1)S(1)} %gather_fusion, bf16[320,128,128]{2,1,0:T(8,128)(2,1)} %get-tuple-element.465, s32[]{:T(128)S(6)} %select_n.62), kind=kOutput, calls=%fused_computation.4.clone.1 | convolution fusion | flops 268435456 | bytes 8388612 | tf_op jit(solution)/shard_map/while/body/eval_jaxpr/tab,tbf->taf/dot_general | solution.py:51
  342.3 8.8 %scatter_fusion = f32[5,128,128]{2,1,0:T(8,128)S(1)} fusion(f32[5,128,128]{2,1,0:T(8,128)S(1)} %broadcast.105, s32[64]{0:T(128)S(1)} %get-tuple-element.426, f32[64,128,128]{2,1,0:T(8,128)} %fusion.22), kind=kCustom, calls=%fused_computation.2.clone.clone.1 | custom fusion | flops 1048576 | bytes 12583168 | tf_op jit(solution)/shard_map/while/body/eval_jaxpr/scatter-add | solution.py:55
  352.9 4.2 %fusion.22 = f32[64,128,128]{2,1,0:T(8,128)} fusion(bf16[64,128,128]{2,1,0:T(8,128)(2,1)S(1)} %gather_fusion, bf16[320,128,128]{2,1,0:T(8,128)(2,1)} %get-tuple-element.465, s32[]{:T(128)S(6)} %select_n.62), kind=kOutput, calls=%fused_computation.4.clone.1 | convolution fusion | flops 268435456 | bytes 8388612 | tf_op jit(solution)/shard_map/while/body/eval_jaxpr/tab,tbf->taf/dot_general | solution.py:51
  357.2 8.8 %scatter_fusion = f32[5,128,128]{2,1,0:T(8,128)S(1)} fusion(f32[5,128,128]{2,1,0:T(8,128)S(1)} %broadcast.105, s32[64]{0:T(128)S(1)} %get-tuple-element.426, f32[64,128,128]{2,1,0:T(8,128)} %fusion.22), kind=kCustom, calls=%fused_computation.2.clone.clone.1 | custom fusion | flops 1048576 | bytes 12583168 | tf_op jit(solution)/shard_map/while/body/eval_jaxpr/scatter-add | solution.py:55
  367.7 4.2 %fusion.22 = f32[64,128,128]{2,1,0:T(8,128)} fusion(bf16[64,128,128]{2,1,0:T(8,128)(2,1)S(1)} %gather_fusion, bf16[320,128,128]{2,1,0:T(8,128)(2,1)} %get-tuple-element.465, s32[]{:T(128)S(6)} %select_n.62), kind=kOutput, calls=%fused_computation.4.clone.1 | convolution fusion | flops 268435456 | bytes 8388612 | tf_op jit(solution)/shard_map/while/body/eval_jaxpr/tab,tbf->taf/dot_general | solution.py:51
  372.0 8.8 %scatter_fusion = f32[5,128,128]{2,1,0:T(8,128)S(1)} fusion(f32[5,128,128]{2,1,0:T(8,128)S(1)} %broadcast.105, s32[64]{0:T(128)S(1)} %get-tuple-element.426, f32[64,128,128]{2,1,0:T(8,128)} %fusion.22), kind=kCustom, calls=%fused_computation.2.clone.clone.1 | custom fusion | flops 1048576 | bytes 12583168 | tf_op jit(solution)/shard_map/while/body/eval_jaxpr/scatter-add | solution.py:55
  382.6 4.2 %fusion.22 = f32[64,128,128]{2,1,0:T(8,128)} fusion(bf16[64,128,128]{2,1,0:T(8,128)(2,1)S(1)} %gather_fusion, bf16[320,128,128]{2,1,0:T(8,128)(2,1)} %get-tuple-element.465, s32[]{:T(128)S(6)} %select_n.62), kind=kOutput, calls=%fused_computation.4.clone.1 | convolution fusion | flops 268435456 | bytes 8388612 | tf_op jit(solution)/shard_map/while/body/eval_jaxpr/tab,tbf->taf/dot_general | solution.py:51
  386.8 8.8 %scatter_fusion = f32[5,128,128]{2,1,0:T(8,128)S(1)} fusion(f32[5,128,128]{2,1,0:T(8,128)S(1)} %broadcast.105, s32[64]{0:T(128)S(1)} %get-tuple-element.426, f32[64,128,128]{2,1,0:T(8,128)} %fusion.22), kind=kCustom, calls=%fused_computation.2.clone.clone.1 | custom fusion | flops 1048576 | bytes 12583168 | tf_op jit(solution)/shard_map/while/body/eval_jaxpr/scatter-add | solution.py:55
  399.8 7.2 %reduce-scatter.3.cloned.1.call-done = f32[256,128]{1,0:T(8,128)} async-done(((f32[512,128]{1,0:T(8,128)}), f32[256,128]{1,0:T(8,128)}) %reduce-scatter.3.cloned.1.call-update) | async-done | bytes 131088 | tf_op jit(solution)/shard_map/reduce_scatter | solution.py:64
  (75 shorter events, 32.2 us)
Async XLA Ops:
  7.2 312.1 %copy-start = (bf16[256,128]{1,0:T(8,128)(2,1)S(1)}, bf16[256,128]{1,0:T(8,128)(2,1)}, u32[]{:S(2)}) copy-start(bf16[256,128]{1,0:T(8,128)(2,1)} %param.12) | copy-start | bytes 196612
  7.2 175.6 %reduce-scatter.5.cloned.1.call-start = ((), (), s32[]{:S(2)}) async-start(), calls=%async_computation.4 | async-start | bytes 2228224 | tf_op jit(solution)/shard_map/reduce_scatter | solution.py:88
  8.6 14.4 %copy-start.3 = (bf16[256,128]{1,0:T(8,128)(2,1)S(1)}, bf16[256,128]{1,0:T(8,128)(2,1)}, u32[]{:S(2)}) copy-start(bf16[256,128]{1,0:T(8,128)(2,1)} %param.17) | copy-start | bytes 196612
  119.1 63.7 %copy-start.2 = (bf16[256,256]{1,0:T(8,128)(2,1)S(1)}, bf16[256,256]{1,0:T(8,128)(2,1)}, u32[]{:S(2)}) copy-start(bf16[256,256]{1,0:T(8,128)(2,1)} %param.11) | copy-start | bytes 393220
  119.1 154.9 %all-reduce.3.cloned.1.call-start = ((), (), s32[]{:S(2)}) async-start(), calls=%async_computation.5 | async-start | bytes 262144 | tf_op jit(solution)/shard_map/psum | solution.py:12
  184.6 134.6 %all-gather.2.cloned.1.call-start = ((), (), s32[]{:S(2)}) async-start(), calls=%async_computation.2 | async-start | bytes 2228224 | tf_op jit(solution)/shard_map/all_gather | solution.py:35
  185.3 212.9 %all-reduce.5.cloned.1.call-start = ((), (), s32[]{:S(2)}) async-start(), calls=%async_computation.6 | async-start | bytes 262144 | tf_op jit(solution)/shard_map/psum | solution.py:12
  274.0 133.0 %reduce-scatter.3.cloned.1.call-start = ((), (), s32[]{:S(2)}) async-start(), calls=%async_computation.3 | async-start | bytes 393216 | tf_op jit(solution)/shard_map/reduce_scatter | solution.py:64
  395.7 0.7 copy-start.1
Sparse Core Ops, SparseCore 0:
  119.3 63.4 reduce-scatter.4
  186.8 87.1 all-reduce.2
  276.2 42.9 all-gather.1
  321.3 20.2 all-reduce.4
  396.5 10.4 reduce-scatter.2
